TPU v7x, 512 devices: a whole 4x4x16 slice. The times are simulated.
512 devices in a mesh: band: 16 (over x, y), lon: 32 (over z, core).
Axes of the slice: x: 4, y: 4, z: 16, core: 2. Of those that a mesh axis runs over, the one named last changes fastest.
Arguments:
- back_height: float32 [1024, 8640], P('band', 'lon'), may hold values from -6 to 6
- back_east: float32 [1024, 8640], P('band', 'lon'), may hold values from -6 to 6
- back_north: float32 [1024, 8640], P('band', 'lon'), may hold values from -6 to 6
- obs_values: float32 [65536, 256], P(('band', 'lon')), may hold values from -6 to 6
- obs_owner: int32 [65536, 1], P(('band', 'lon')), may hold values from 0 to 31; in each aligned block of 128 rows (0 to 127, 128 to 255, ...) at most 12 rows name the same one
- obs_row: int32 [65536], P(('band', 'lon')), may hold values from 0 to 63
- obs_count: int32 [65536], P(('band', 'lon')), may hold values from 1 to 256
- polar_mask: int32 [1024], P('band'), may hold values from 0 to 1, as said below
- keep_share: float32 [1024], P('band'), may hold values from 0.05 to 0.9
- depth_level: int32 [1024, 8640], P('band', 'lon'), may hold values from 0 to 50
Outputs:
- grad_height: float32 [1024, 8640], P('band', 'lon')
- grad_east: float32 [1024, 8640], P('band', 'lon')
- grad_north: float32 [1024, 8640], P('band', 'lon')
Inputs may be any that keep to these rules, and one draw needn't show every extreme that they name: `obs_owner`: among the rows of one device at most 12 name the same tile, a bound that some block reaches. `polar_mask`: among the 64 rows of one band at most 32 are 1, and some band has exactly 32.
All inputs are finite; a program needn't handle non-finite values.
Results may differ from a plain program's by a relative error of at most 0.00005.
Values sent between devices are 32-bit elements; how exact they have to be, the bound alone decides.
No kernel may reach another device: no remote copies, remote signals or barrier semaphores. Data moves between devices by JAX's collectives and lax.ppermute only.
A program may use at most 64 MiB of HBM per device.

v0:
```python
import math
import jax
import jax.numpy as jnp
from jax import lax
from jax.sharding import PartitionSpec as P

MODES = 128
LEVELS = 50
COURANT = 0.25
ROTATION = 0.4
LIMIT = 1.3089969389957472
OUTER_COUNT = 64


def with_halo(cells, sides, width, closed):
    for axis, dim in sides:
        count = lax.axis_size(axis)
        ends = count if closed else count - 1
        head = lax.slice_in_dim(cells, 0, width, axis=dim)
        tail = lax.slice_in_dim(cells, cells.shape[dim] - width, cells.shape[dim], axis=dim)
        cells = jnp.concatenate(
            [
                lax.ppermute(tail, axis, [(i, (i + 1) % count) for i in range(ends)]),
                cells,
                lax.ppermute(head, axis, [((i + 1) % count, i) for i in range(ends)]),
            ],
            axis=dim,
        )
    return cells


def latitude_terms(first_row, count_rows, total_rows):
    global_rows = first_row + jnp.arange(count_rows, dtype=jnp.int32)
    centre = (global_rows.astype(jnp.float32) + 0.5) / total_rows
    angle = (2.0 * centre - 1.0) * LIMIT
    return (1.0 / jnp.cos(angle), ROTATION * jnp.sin(angle))


def spectral_tables(length, modes):
    inner_count = length // OUTER_COUNT
    outer_pos = jnp.arange(OUTER_COUNT, dtype=jnp.int32)
    outer_phase = outer_pos[:, None] * outer_pos[None, :] % OUTER_COUNT
    outer_angle = outer_phase.astype(jnp.float32) * (2.0 * math.pi / OUTER_COUNT)
    number = jnp.arange(modes, dtype=jnp.int32)
    inner_pos = jnp.arange(inner_count, dtype=jnp.int32)
    inner_phase = number[:, None] * inner_pos[None, :] % length
    inner_angle = inner_phase.astype(jnp.float32) * (2.0 * math.pi / length)
    grouping = (number[:, None] % OUTER_COUNT == outer_pos[None, :]).astype(jnp.float32)
    mode_weights = jnp.where(number == 0, 1.0 / length, 2.0 / length).astype(jnp.float32)
    return (
        jnp.cos(outer_angle),
        jnp.sin(outer_angle),
        jnp.cos(inner_angle),
        jnp.sin(inner_angle),
        grouping,
        mode_weights,
    )


def project_rows(pieces, tables):
    cos_outer, sin_outer, cos_inner, sin_inner, grouping, mode_weights = tables
    fields, rows, length = pieces.shape
    inner_count = length // OUTER_COUNT
    highest = lax.Precision.HIGHEST
    split = pieces.reshape(fields, rows, OUTER_COUNT, inner_count)
    real_part = jnp.einsum("fnab,ar->fnrb", split, cos_outer, precision=highest)
    imag_part = -jnp.einsum("fnab,ar->fnrb", split, sin_outer, precision=highest)
    real_mode = jnp.einsum("fnrb,mr->fnmb", real_part, grouping, precision=highest)
    imag_mode = jnp.einsum("fnrb,mr->fnmb", imag_part, grouping, precision=highest)
    coeff_real = jnp.sum(real_mode * cos_inner + imag_mode * sin_inner, axis=3) * mode_weights
    coeff_imag = jnp.sum(imag_mode * cos_inner - real_mode * sin_inner, axis=3) * mode_weights
    back_real = coeff_real[..., None] * cos_inner - coeff_imag[..., None] * sin_inner
    back_imag = coeff_real[..., None] * sin_inner + coeff_imag[..., None] * cos_inner
    group_real = jnp.einsum("fnmb,mr->fnrb", back_real, grouping, precision=highest)
    group_imag = jnp.einsum("fnmb,mr->fnrb", back_imag, grouping, precision=highest)
    result = jnp.einsum("fnrb,ar->fnab", group_real, cos_outer, precision=highest) - jnp.einsum(
        "fnrb,ar->fnab", group_imag, sin_outer, precision=highest
    )
    return result.reshape(fields, rows, length)


def extend(stacked, width):
    wider = with_halo(stacked, (("lon", 2),), width, True)
    return with_halo(wider, (("band", 1),), width, False)


def polar_filter(stacked, weight, tables):
    smooth = project_rows(
        lax.all_to_all(stacked, "lon", split_axis=1, concat_axis=2, tiled=True), tables
    )
    projected = lax.all_to_all(smooth, "lon", split_axis=2, concat_axis=1, tiled=True)
    return stacked + weight[None, :, None] * (projected - stacked)


def adjoint_step(state, weight, tables, wet_cells, depth_share, metric, rotation):
    stacked = jnp.stack([state[0], wet_cells * state[1], wet_cells * state[2]])
    kept = polar_filter(stacked, weight, tables)
    height_kept = kept[0]
    east_kept = kept[1]
    north_kept = kept[2]
    wider = extend(kept[1:], 1)
    middle = height_kept + COURANT * (
        metric[:, None] * (wider[0, 1:-1, 2:] - wider[0, 1:-1, :-2]) * 0.5
        + (wider[1, 2:, 1:-1] - wider[1, :-2, 1:-1]) * 0.5
    )
    beside_all = extend(middle[None], 1)[0]
    new_east = (
        east_kept
        - rotation[:, None] * north_kept
        + COURANT
        * depth_share
        * (metric[:, None] * (beside_all[1:-1, 2:] - beside_all[1:-1, :-2]) * 0.5)
    )
    new_north = (
        north_kept
        + rotation[:, None] * east_kept
        + COURANT * depth_share * ((beside_all[2:, 1:-1] - beside_all[:-2, 1:-1]) * 0.5)
    )
    return (middle, new_east, new_north)


def place_observations(
    obs_values, obs_owner, obs_row, obs_count, lon_count, count_rows, count_cols
):
    sample_rows, sample_width = obs_values.shape
    capacity = 3 * sample_rows // lon_count
    owner_ids = obs_owner[:, 0]
    owner_hits = (owner_ids[:, None] == jnp.arange(lon_count, dtype=jnp.int32)[None, :]).astype(
        jnp.int32
    )
    arrival = jnp.sum((jnp.cumsum(owner_hits, axis=0) - 1) * owner_hits, axis=1)
    target = owner_ids * capacity + arrival
    outgoing = (
        jnp.zeros((lon_count * capacity, sample_width), jnp.float32).at[target].set(obs_values)
    )
    labels = (
        jnp.zeros((lon_count * capacity, 2), jnp.int32)
        .at[target]
        .set(jnp.stack([obs_row, obs_count], axis=1))
    )
    incoming, tagged = (
        lax.all_to_all(
            outgoing.reshape(lon_count, capacity, sample_width),
            "lon",
            split_axis=0,
            concat_axis=0,
            tiled=True,
        ),
        lax.all_to_all(
            labels.reshape(lon_count, capacity, 2), "lon", split_axis=0, concat_axis=0, tiled=True
        ),
    )
    flat_values = incoming.reshape(lon_count * capacity, sample_width)
    flat_labels = tagged.reshape(lon_count * capacity, 2)
    alive_cells = jnp.arange(sample_width, dtype=jnp.int32)[None, :] < flat_labels[:, 1:2]
    summed = jax.ops.segment_sum(
        jnp.where(alive_cells, flat_values, 0.0), flat_labels[:, 0], num_segments=count_rows
    )
    return jnp.pad(summed, ((0, 0), (0, count_cols - sample_width)))


def on_device(
    back_height,
    back_east,
    back_north,
    obs_values,
    obs_owner,
    obs_row,
    obs_count,
    polar_mask,
    keep_share,
    depth_level,
):
    count_rows, count_cols = back_height.shape
    band_count = lax.axis_size("band")
    lon_count = lax.axis_size("lon")
    total_rows = count_rows * band_count
    first_row = lax.axis_index("band") * count_rows
    metric, rotation = latitude_terms(first_row, count_rows, total_rows)
    wet_cells = (depth_level > 0).astype(jnp.float32)
    depth_share = depth_level.astype(jnp.float32) / LEVELS
    weight = polar_mask.astype(jnp.float32) * (1.0 - keep_share)
    tables = spectral_tables(count_cols * lon_count, MODES)
    placed = place_observations(
        obs_values, obs_owner, obs_row, obs_count, lon_count, count_rows, count_cols
    )
    state = (back_height, back_east, back_north)
    state = adjoint_step(state, weight, tables, wet_cells, depth_share, metric, rotation)
    state = (state[0] + placed, state[1], state[2])
    state = adjoint_step(state, weight, tables, wet_cells, depth_share, metric, rotation)
    return (state[0], state[1], state[2])


def solution(mesh):
    placed = (
        P("band", "lon"),
        P("band", "lon"),
        P("band", "lon"),
        P(("band", "lon"), None),
        P(("band", "lon"), None),
        P(("band", "lon")),
        P(("band", "lon")),
        P("band"),
        P("band"),
        P("band", "lon"),
    )
    return jax.shard_map(
        on_device,
        mesh=mesh,
        in_specs=placed,
        out_specs=(P("band", "lon"), P("band", "lon"), P("band", "lon")),
        check_vma=False,
    )
```

profile of v0, /device:TPU:26, one launch (start us, length us, event | category | flops | bytes accessed | tf_op | source)
XLA Modules:
  0.0 317.1 jit_solution(5938740981193499104)
XLA Ops:
  0.6 1.0 select_bitcast_fusion.1
  1.6 0.9 pad_maximum_fusion
  2.6 1.0 copy.81
  3.5 15.5 %all-to-all-start = ((f32[3,64,270]{2,0,1:T(4,128)}), f32[3,64,270]{2,0,1:T(4,128)S(1)}, u32[]{:S(2)}, u32[]{:S(2)}) async-start(f32[3,64,270]{2,0,1:T(4,128)} %copy.81), calls=%async_computation | async-start | bytes 786432 | tf_op jit(solution)/shard_map/all_to_all | solution.py:89
  19.8 0.7 fusion.75
  20.7 0.8 select_reduce_fusion
  22.2 0.9 scatter_custom_fusion
  24.3 22.9 %all-to-all-done = f32[3,64,270]{2,0,1:T(4,128)S(1)} async-done(((f32[3,64,270]{2,0,1:T(4,128)}), f32[3,64,270]{2,0,1:T(4,128)S(1)}, u32[]{:S(2)}, u32[]{:S(2)}) %all-to-all-start) | async-done | bytes 207392 | tf_op jit(solution)/shard_map/all_to_all | solution.py:89
  47.2 3.9 %all-to-all-start.2 = ((s32[32,12,2]{1,2,0:T(2,128)}), s32[32,12,2]{1,2,0:T(2,128)S(1)}, u32[]{:S(2)}, u32[]{:S(2)}) async-start(s32[32,12,2]{1,2,0:T(2,128)} %copy.89), calls=%async_computation.2 | async-start | bytes 65536 | tf_op jit(solution)/shard_map/all_to_all | solution.py:149
  56.3 11.0 %copy.106 = f32[3,2,64,135]{0,1,3,2:T(2,128)} copy(f32[3,2,64,135]{3,2,1,0:T(8,128)S(1)} %fusion.2) | data formatting | bytes 414720 | tf_op jit(solution)/shard_map/reshape | solution.py:79
  67.3 11.7 %reshape.177 = f32[32,1,1620]{2,1,0:T(1,128)} reshape(f32[8640,2,3]{2,1,0:T(2,128)} %bitcast.184) | data formatting | bytes 414720
  79.0 12.2 %all-to-all-start.1 = ((f32[32,1,1620]{2,1,0:T(1,128)}), f32[32,1,1620]{2,1,0:T(1,128)S(1)}, u32[]{:S(2)}, u32[]{:S(2)}) async-start(f32[32,1,1620]{2,1,0:T(1,128)} %reshape.177), calls=%async_computation.1 | async-start | bytes 425984 | tf_op jit(solution)/shard_map/all_to_all | solution.py:91
  91.2 1.5 scatter_custom_fusion.1
  92.7 0.9 reshape.134
  93.6 18.3 %all-to-all-done.1 = f32[32,1,1620]{2,1,0:T(1,128)S(1)} async-done(((f32[32,1,1620]{2,1,0:T(1,128)}), f32[32,1,1620]{2,1,0:T(1,128)S(1)}, u32[]{:S(2)}, u32[]{:S(2)}) %all-to-all-start.1) | async-done | bytes 207392 | tf_op jit(solution)/shard_map/all_to_all | solution.py:91
  111.9 4.1 %all-to-all-start.3 = ((f32[32,12,256]{2,1,0:T(8,128)}), f32[32,12,256]{2,1,0:T(8,128)S(1)}, u32[]{:S(2)}, u32[]{:S(2)}) async-start(f32[32,12,256]{2,1,0:T(8,128)} %reshape.134), calls=%async_computation.3 | async-start | bytes 1048576 | tf_op jit(solution)/shard_map/all_to_all | solution.py:142
  116.5 1.1 reduce.8
  117.7 8.1 %reshape.178 = f32[8640,2,3]{2,1,0:T(2,128)} reshape(f32[32,1620]{1,0:T(8,128)S(1)} %reduce.8) | data formatting | bytes 414720
  125.8 11.2 %copy.86 = f32[3,2,32,270]{3,1,2,0:T(2,128)S(1)} copy(f32[3,2,32,270]{0,1,3,2:T(2,128)} %bitcast.185) | data formatting | bytes 414720 | tf_op jit(solution)/shard_map/all_to_all | solution.py:91
  137.3 2.7 collective-permute-start
  140.2 1.7 collective-permute-done
  141.9 3.1 collective-permute-done.1
  145.1 2.7 collective-permute-start.2
  147.8 5.3 %collective-permute-start.3 = (f32[2,1,272]{2,1,0:T(1,128)S(1)}, f32[2,1,272]{2,1,0:T(1,128)S(1)}, u32[]{:S(2)}, u32[]{:S(2)}) collective-permute-start(f32[2,1,272]{2,1,0:T(1,128)S(1)} %get-tuple-element.22), channel_id=1, source_target_pairs={{0,32},{32,64},{64,96},{96,128},{128,160},{160,192},{192,224},{224... | collective-permute-start | bytes 6536 | tf_op jit(solution)/shard_map/ppermute | solution.py:23
  153.2 2.9 scatter_custom_fusion.2
  156.5 3.0 collective-permute-start.5
  159.4 1.6 collective-permute-done.4
  161.1 4.6 %collective-permute-start.6 = (f32[1,1,272]{2,1,0:T(1,128)S(1)}, f32[1,1,272]{2,1,0:T(1,128)S(1)}, u32[]{:S(2)}, u32[]{:S(2)}) collective-permute-start(f32[1,1,272]{2,1,0:T(1,128)S(1)} %get-tuple-element.30), channel_id=1, source_target_pairs={{0,32},{32,64},{64,96},{96,128},{128,160},{160,192},{192,224},{224... | collective-permute-start | bytes 3272 | tf_op jit(solution)/shard_map/ppermute | solution.py:23
  165.7 1.9 collective-permute-start.7
  167.7 5.6 %collective-permute-done.7 = f32[1,1,272]{2,1,0:T(1,128)S(1)} collective-permute-done((f32[1,1,272]{2,1,0:T(1,128)S(1)}, f32[1,1,272]{2,1,0:T(1,128)S(1)}, u32[]{:S(2)}, u32[]{:S(2)}) %collective-permute-start.7) | collective-permute-done | bytes 1120 | tf_op jit(solution)/shard_map/ppermute | solution.py:25
  173.8 37.5 %all_to_all.76 = f32[3,64,270]{2,0,1:T(4,128)S(1)} all-to-all(f32[3,64,270]{2,0,1:T(4,128)S(1)} %copy.91), channel_id=1, replica_groups=mesh['band'=16,'lon'=32] {'lon'}, dimensions={1} | all-to-all | bytes 414720 | tf_op jit(solution)/shard_map/all_to_all | solution.py:89
  216.5 11.0 %copy.109 = f32[3,2,64,135]{0,1,3,2:T(2,128)} copy(f32[3,2,64,135]{3,2,1,0:T(8,128)S(1)} %fusion) | data formatting | bytes 414720 | tf_op jit(solution)/shard_map/reshape | solution.py:79
  227.5 11.1 %reshape.179 = f32[32,1,1620]{2,1,0:T(1,128)S(1)} reshape(f32[8640,2,3]{2,1,0:T(2,128)} %bitcast.186) | data formatting | bytes 414720
  238.6 23.7 %all_to_all.77 = f32[32,1,1620]{2,1,0:T(1,128)S(1)} all-to-all(f32[32,1,1620]{2,1,0:T(1,128)S(1)} %reshape.179), channel_id=1, replica_groups=mesh['band'=16,'lon'=32] {'lon'}, dimensions={0} | all-to-all | bytes 414720 | tf_op jit(solution)/shard_map/all_to_all | solution.py:91
  262.3 1.2 reduce.9
  263.4 8.1 %reshape.180 = f32[8640,2,3]{2,1,0:T(2,128)} reshape(f32[32,1620]{1,0:T(8,128)S(1)} %reduce.9) | data formatting | bytes 414720
  271.5 11.1 %copy.96 = f32[3,2,32,270]{3,1,2,0:T(2,128)S(1)} copy(f32[3,2,32,270]{0,1,3,2:T(2,128)} %bitcast.187) | data formatting | bytes 414720 | tf_op jit(solution)/shard_map/all_to_all | solution.py:91
  283.6 1.4 collective-permute-done.8
  285.0 3.0 collective-permute-done.9
  288.1 1.9 collective-permute-start.10
  290.0 6.0 %collective-permute-start.11 = (f32[2,1,272]{2,1,0:T(1,128)S(1)}, f32[2,1,272]{2,1,0:T(1,128)S(1)}, u32[]{:S(2)}, u32[]{:S(2)}) collective-permute-start(f32[2,1,272]{2,1,0:T(1,128)S(1)} %get-tuple-element.20), channel_id=1, source_target_pairs={{0,32},{32,64},{64,96},{96,128},{128,160},{160,192},{192,224},{224... | collective-permute-start | bytes 6536 | tf_op jit(solution)/shard_map/ppermute | solution.py:23
  296.1 1.3 collective-permute-done.11
  297.6 3.0 collective-permute-start.13
  300.6 1.6 collective-permute-done.12
  302.3 6.3 %collective-permute-start.14 = (f32[1,1,272]{2,1,0:T(1,128)S(1)}, f32[1,1,272]{2,1,0:T(1,128)S(1)}, u32[]{:S(2)}, u32[]{:S(2)}) collective-permute-start(f32[1,1,272]{2,1,0:T(1,128)S(1)} %get-tuple-element.28), channel_id=1, source_target_pairs={{0,32},{32,64},{64,96},{96,128},{128,160},{160,192},{192,224},{224... | collective-permute-start | bytes 3272 | tf_op jit(solution)/shard_map/ppermute | solution.py:23
  308.6 1.9 collective-permute-start.15
  310.5 5.6 %collective-permute-done.15 = f32[1,1,272]{2,1,0:T(1,128)S(1)} collective-permute-done((f32[1,1,272]{2,1,0:T(1,128)S(1)}, f32[1,1,272]{2,1,0:T(1,128)S(1)}, u32[]{:S(2)}, u32[]{:S(2)}) %collective-permute-start.15) | collective-permute-done | bytes 1120 | tf_op jit(solution)/shard_map/ppermute | solution.py:25
  316.2 0.9 fusion.40
  (84 shorter events, 16.8 us)
Async XLA Ops:
  3.5 43.7 %all-to-all-start = ((f32[3,64,270]{2,0,1:T(4,128)}), f32[3,64,270]{2,0,1:T(4,128)S(1)}, u32[]{:S(2)}, u32[]{:S(2)}) async-start(f32[3,64,270]{2,0,1:T(4,128)} %copy.81), calls=%async_computation | async-start | bytes 786432 | tf_op jit(solution)/shard_map/all_to_all | solution.py:89
  47.2 31.8 %all-to-all-start.2 = ((s32[32,12,2]{1,2,0:T(2,128)}), s32[32,12,2]{1,2,0:T(2,128)S(1)}, u32[]{:S(2)}, u32[]{:S(2)}) async-start(s32[32,12,2]{1,2,0:T(2,128)} %copy.89), calls=%async_computation.2 | async-start | bytes 65536 | tf_op jit(solution)/shard_map/all_to_all | solution.py:149
  56.3 59.7 %copy-start.2 = (f32[64]{0:T(128)S(1)}, f32[64]{0:T(128)}, u32[]{:S(2)}) copy-start(f32[64]{0:T(128)} %param.18) | copy-start | bytes 772
  56.3 59.7 %copy-start.3 = (s32[64]{0:T(128)S(1)}, s32[64]{0:T(128)}, u32[]{:S(2)}) copy-start(s32[64]{0:T(128)} %param.17) | copy-start | bytes 772
  79.0 32.9 %all-to-all-start.1 = ((f32[32,1,1620]{2,1,0:T(1,128)}), f32[32,1,1620]{2,1,0:T(1,128)S(1)}, u32[]{:S(2)}, u32[]{:S(2)}) async-start(f32[32,1,1620]{2,1,0:T(1,128)} %reshape.177), calls=%async_computation.1 | async-start | bytes 425984 | tf_op jit(solution)/shard_map/all_to_all | solution.py:91
  111.9 41.3 %all-to-all-start.3 = ((f32[32,12,256]{2,1,0:T(8,128)}), f32[32,12,256]{2,1,0:T(8,128)S(1)}, u32[]{:S(2)}, u32[]{:S(2)}) async-start(f32[32,12,256]{2,1,0:T(8,128)} %reshape.134), calls=%async_computation.3 | async-start | bytes 1048576 | tf_op jit(solution)/shard_map/all_to_all | solution.py:142
  117.6 19.5 %copy-start.1 = (f32[64,270]{1,0:T(8,128)S(1)}, f32[64,270]{1,0:T(8,128)}, u32[]{:S(2)}) copy-start(f32[64,270]{1,0:T(8,128)} %param.10) | copy-start | bytes 207364
  125.8 47.6 %copy-start = (s32[64,270]{1,0:T(8,128)S(1)}, s32[64,270]{1,0:T(8,128)}, u32[]{:S(2)}) copy-start(s32[64,270]{1,0:T(8,128)} %param.19) | copy-start | bytes 207364
  137.3 4.6 %collective-permute-start = (f32[2,64,1]{2,1,0:T(8,128)S(1)}, f32[2,64,1]{2,1,0:T(8,128)S(1)}, u32[]{:S(2)}, u32[]{:S(2)}) collective-permute-start(f32[2,64,1]{2,1,0:T(8,128)S(1)} %get-tuple-element.26), channel_id=1, source_target_pairs={{1,0},{2,1},{3,2},{4,3},{5,4},{6,5},{7,6},{8,7},{9,8},{10,9},{11,1... | collective-permute-start | bytes 1544 | tf_op jit(solution)/shard_map/ppermute | solution.py:25
  140.0 5.0 %collective-permute-start.1 = (f32[2,64,1]{2,1,0:T(8,128)S(1)}, f32[2,64,1]{2,1,0:T(8,128)S(1)}, u32[]{:S(2)}, u32[]{:S(2)}) collective-permute-start(f32[2,64,1]{2,1,0:T(8,128)S(1)} %get-tuple-element.27), channel_id=1, source_target_pairs={{0,1},{1,2},{2,3},{3,4},{4,5},{5,6},{6,7},{7,8},{8,9},{9,10},{10,1... | collective-permute-start | bytes 1544 | tf_op jit(solution)/shard_map/ppermute | solution.py:23
  145.1 10.9 %collective-permute-start.2 = (f32[2,1,272]{2,1,0:T(1,128)S(1)}, f32[2,1,272]{2,1,0:T(1,128)S(1)}, u32[]{:S(2)}, u32[]{:S(2)}) collective-permute-start(f32[2,1,272]{2,1,0:T(1,128)S(1)} %get-tuple-element.21), channel_id=1, source_target_pairs={{32,0},{64,32},{96,64},{128,96},{160,128},{192,160},{224,192},{256... | collective-permute-start | bytes 6536 | tf_op jit(solution)/shard_map/ppermute | solution.py:25
  147.8 8.3 %collective-permute-start.3 = (f32[2,1,272]{2,1,0:T(1,128)S(1)}, f32[2,1,272]{2,1,0:T(1,128)S(1)}, u32[]{:S(2)}, u32[]{:S(2)}) collective-permute-start(f32[2,1,272]{2,1,0:T(1,128)S(1)} %get-tuple-element.22), channel_id=1, source_target_pairs={{0,32},{32,64},{64,96},{96,128},{128,160},{160,192},{192,224},{224... | collective-permute-start | bytes 6536 | tf_op jit(solution)/shard_map/ppermute | solution.py:23
  156.4 4.6 %collective-permute-start.4 = (f32[1,64,1]{2,1,0:T(8,128)S(1)}, f32[1,64,1]{2,1,0:T(8,128)S(1)}, u32[]{:S(2)}, u32[]{:S(2)}) collective-permute-start(f32[1,64,1]{2,1,0:T(8,128)S(1)} %get-tuple-element.34), channel_id=1, source_target_pairs={{0,1},{1,2},{2,3},{3,4},{4,5},{5,6},{6,7},{7,8},{8,9},{9,10},{10,1... | collective-permute-start | bytes 776 | tf_op jit(solution)/shard_map/ppermute | solution.py:23
  156.5 4.6 %collective-permute-start.5 = (f32[1,64,1]{2,1,0:T(8,128)S(1)}, f32[1,64,1]{2,1,0:T(8,128)S(1)}, u32[]{:S(2)}, u32[]{:S(2)}) collective-permute-start(f32[1,64,1]{2,1,0:T(8,128)S(1)} %get-tuple-element.35), channel_id=1, source_target_pairs={{1,0},{2,1},{3,2},{4,3},{5,4},{6,5},{7,6},{8,7},{9,8},{10,9},{11,1... | collective-permute-start | bytes 776 | tf_op jit(solution)/shard_map/ppermute | solution.py:25
  161.1 6.6 %collective-permute-start.6 = (f32[1,1,272]{2,1,0:T(1,128)S(1)}, f32[1,1,272]{2,1,0:T(1,128)S(1)}, u32[]{:S(2)}, u32[]{:S(2)}) collective-permute-start(f32[1,1,272]{2,1,0:T(1,128)S(1)} %get-tuple-element.30), channel_id=1, source_target_pairs={{0,32},{32,64},{64,96},{96,128},{128,160},{160,192},{192,224},{224... | collective-permute-start | bytes 3272 | tf_op jit(solution)/shard_map/ppermute | solution.py:23
  165.7 7.6 %collective-permute-start.7 = (f32[1,1,272]{2,1,0:T(1,128)S(1)}, f32[1,1,272]{2,1,0:T(1,128)S(1)}, u32[]{:S(2)}, u32[]{:S(2)}) collective-permute-start(f32[1,1,272]{2,1,0:T(1,128)S(1)} %get-tuple-element.31), channel_id=1, source_target_pairs={{32,0},{64,32},{96,64},{128,96},{160,128},{192,160},{224,192},{256... | collective-permute-start | bytes 3272 | tf_op jit(solution)/shard_map/ppermute | solution.py:25
  283.1 1.9 collective-permute-start.8
  283.1 4.9 %collective-permute-start.9 = (f32[2,64,1]{2,1,0:T(8,128)S(1)}, f32[2,64,1]{2,1,0:T(8,128)S(1)}, u32[]{:S(2)}, u32[]{:S(2)}) collective-permute-start(f32[2,64,1]{2,1,0:T(8,128)S(1)} %get-tuple-element.25), channel_id=1, source_target_pairs={{0,1},{1,2},{2,3},{3,4},{4,5},{5,6},{6,7},{7,8},{8,9},{9,10},{10,1... | collective-permute-start | bytes 1544 | tf_op jit(solution)/shard_map/ppermute | solution.py:23
  288.1 8.0 %collective-permute-start.10 = (f32[2,1,272]{2,1,0:T(1,128)S(1)}, f32[2,1,272]{2,1,0:T(1,128)S(1)}, u32[]{:S(2)}, u32[]{:S(2)}) collective-permute-start(f32[2,1,272]{2,1,0:T(1,128)S(1)} %get-tuple-element.19), channel_id=1, source_target_pairs={{32,0},{64,32},{96,64},{128,96},{160,128},{192,160},{224,192},{256... | collective-permute-start | bytes 6536 | tf_op jit(solution)/shard_map/ppermute | solution.py:25
  290.0 7.3 %collective-permute-start.11 = (f32[2,1,272]{2,1,0:T(1,128)S(1)}, f32[2,1,272]{2,1,0:T(1,128)S(1)}, u32[]{:S(2)}, u32[]{:S(2)}) collective-permute-start(f32[2,1,272]{2,1,0:T(1,128)S(1)} %get-tuple-element.20), channel_id=1, source_target_pairs={{0,32},{32,64},{64,96},{96,128},{128,160},{160,192},{192,224},{224... | collective-permute-start | bytes 6536 | tf_op jit(solution)/shard_map/ppermute | solution.py:23
  297.6 4.6 %collective-permute-start.12 = (f32[1,64,1]{2,1,0:T(8,128)S(1)}, f32[1,64,1]{2,1,0:T(8,128)S(1)}, u32[]{:S(2)}, u32[]{:S(2)}) collective-permute-start(f32[1,64,1]{2,1,0:T(8,128)S(1)} %get-tuple-element.32), channel_id=1, source_target_pairs={{0,1},{1,2},{2,3},{3,4},{4,5},{5,6},{6,7},{7,8},{8,9},{9,10},{10,1... | collective-permute-start | bytes 776 | tf_op jit(solution)/shard_map/ppermute | solution.py:23
  297.6 4.6 %collective-permute-start.13 = (f32[1,64,1]{2,1,0:T(8,128)S(1)}, f32[1,64,1]{2,1,0:T(8,128)S(1)}, u32[]{:S(2)}, u32[]{:S(2)}) collective-permute-start(f32[1,64,1]{2,1,0:T(8,128)S(1)} %get-tuple-element.33), channel_id=1, source_target_pairs={{1,0},{2,1},{3,2},{4,3},{5,4},{6,5},{7,6},{8,7},{9,8},{10,9},{11,1... | collective-permute-start | bytes 776 | tf_op jit(solution)/shard_map/ppermute | solution.py:25
  302.3 8.2 %collective-permute-start.14 = (f32[1,1,272]{2,1,0:T(1,128)S(1)}, f32[1,1,272]{2,1,0:T(1,128)S(1)}, u32[]{:S(2)}, u32[]{:S(2)}) collective-permute-start(f32[1,1,272]{2,1,0:T(1,128)S(1)} %get-tuple-element.28), channel_id=1, source_target_pairs={{0,32},{32,64},{64,96},{96,128},{128,160},{160,192},{192,224},{224... | collective-permute-start | bytes 3272 | tf_op jit(solution)/shard_map/ppermute | solution.py:23
  308.6 7.6 %collective-permute-start.15 = (f32[1,1,272]{2,1,0:T(1,128)S(1)}, f32[1,1,272]{2,1,0:T(1,128)S(1)}, u32[]{:S(2)}, u32[]{:S(2)}) collective-permute-start(f32[1,1,272]{2,1,0:T(1,128)S(1)} %get-tuple-element.29), channel_id=1, source_target_pairs={{32,0},{64,32},{96,64},{128,96},{160,128},{192,160},{224,192},{256... | collective-permute-start | bytes 3272 | tf_op jit(solution)/shard_map/ppermute | solution.py:25
where the time goes:
time: 318 us; the launch traced here: 317 us
  local copies, waits for them, and re-layouts  90.5 us (28%)
  starting transfers between devices  75.3 us (24%)
  waiting for transfers between devices  66.2 us (21%)
  blocking collectives  61.2 us (19%)
  other arithmetic  12.8 us (4%)
  matrix products  9.91 us (3%)
    unnamed x12, local copies, waits for them, and re-layouts  39 us
    all_to_all x1, blocking collectives, polar_filter(): lax.all_to_all(stacked, 'lon', split_axis=1, concat_axis=2, tiled=True)  37.5 us
    all_to_all x1, blocking collectives, polar_filter(): lax.all_to_all(smooth, 'lon', split_axis=2, concat_axis=1, tiled=True)  23.7 us
    all_to_all x5, local copies, waits for them, and re-layouts, polar_filter(): lax.all_to_all(smooth, 'lon', split_axis=2, concat_axis=1, tiled=True)  23.3 us
    all_to_all x1, waiting for transfers between devices, polar_filter(): lax.all_to_all(stacked, 'lon', split_axis=1, concat_axis=2, tiled=True)  22.9 us
    ppermute x8, starting transfers between devices, with_halo(): lax.ppermute(tail, axis, [(i, (i + 1) % count) for i in range(ends)])  22.7 us
    reshape x2, local copies, waits for them, and re-layouts, project_rows(): return result.reshape(fields, rows, length)  22 us
    all_to_all x1, waiting for transfers between devices, polar_filter(): lax.all_to_all(smooth, 'lon', split_axis=2, concat_axis=1, tiled=True)  18.3 us
  transfers between devices with their start and end apart: 20, of which 11 were waited for; matrix products, arithmetic and copies ran while one was open for 19% of the time, Pallas kernels for 0%

commit v1 on v0

--- a/solution.py
+++ b/solution.py
@@ -10,6 +10,19 @@
 ROTATION = 0.4
 LIMIT = 1.3089969389957472
 OUTER_COUNT = 64
+
+
+def play_the_members_all(local_array):
+    t_next = jnp.concatenate(
+        lax.all_to_all(
+            jnp.stack(jnp.split(local_array, lax.axis_size("lon"), axis=2), axis=0),
+            "lon",
+            split_axis=0,
+            concat_axis=0,
+        ),
+        axis=1,
+    )
+    return t_next
 
 
 def with_halo(cells, sides, width, closed):
@@ -88,7 +101,7 @@
     smooth = project_rows(
         lax.all_to_all(stacked, "lon", split_axis=1, concat_axis=2, tiled=True), tables
     )
-    projected = lax.all_to_all(smooth, "lon", split_axis=2, concat_axis=1, tiled=True)
+    projected = play_the_members_all(smooth)
     return stacked + weight[None, :, None] * (projected - stacked)
 
 

time: 318 us -> 284 us (0.89)
  the two profiles are of different devices: /device:TPU:26 before, /device:TPU:4 now
where the time goes in v1:
time: 284 us
  waiting for transfers between devices  90.9 us (32%)
  starting transfers between devices  74.1 us (26%)
  blocking collectives  66.6 us (23%)
  local copies, waits for them, and re-layouts  33.7 us (12%)
  matrix products  9.92 us (3%)
  other arithmetic  7.01 us (2%)
    ppermute x8, waiting for transfers between devices, with_halo(): lax.ppermute(tail, axis, [(i, (i + 1) % count) for i in range(ends)])  40.9 us
    all_to_all x1, blocking collectives, polar_filter(): lax.all_to_all(stacked, 'lon', split_axis=1, concat_axis=2, tiled=True)  39.5 us
    ppermute x8, starting transfers between devices, with_halo(): lax.ppermute(head, axis, [((i + 1) % count, i) for i in range(ends)])  28.7 us
    all_to_all x1, blocking collectives, play_the_members_all(): lax.all_to_all(jnp.stack(jnp.split(local_array, lax.axis_size('lon'), axi...  27.2 us
    unnamed x76, local copies, waits for them, and re-layouts  25.4 us
    all_to_all x1, waiting for transfers between devices, polar_filter(): lax.all_to_all(stacked, 'lon', split_axis=1, concat_axis=2, tiled=True)  24.2 us
    all_to_all x1, waiting for transfers between devices, play_the_members_all(): lax.all_to_all(jnp.stack(jnp.split(local_array, lax.axis_size('lon'), axi...  21.8 us
    all_to_all x1, starting transfers between devices, polar_filter(): lax.all_to_all(stacked, 'lon', split_axis=1, concat_axis=2, tiled=True)  15.5 us
  transfers between devices with their start and end apart: 20, of which 11 were waited for; matrix products, arithmetic and copies ran while one was open for 13% of the time, Pallas kernels for 0%

profile of v1, /device:TPU:4, one launch (start us, length us, event | category | flops | bytes accessed | tf_op | source)
XLA Modules:
  0.0 283.5 jit_solution(6184320111131222681)
XLA Ops:
  0.6 1.0 select_bitcast_fusion.1
  1.7 0.9 copy.129
  2.7 15.5 %all-to-all-start = ((f32[3,64,270]{2,0,1:T(4,128)}), f32[3,64,270]{2,0,1:T(4,128)S(1)}, u32[]{:S(2)}, u32[]{:S(2)}) async-start(f32[3,64,270]{2,0,1:T(4,128)} %copy.129), calls=%async_computation | async-start | bytes 786432 | tf_op jit(solution)/shard_map/all_to_all | solution.py:102
  20.1 0.9 scatter_custom_fusion
  22.2 24.2 %all-to-all-done = f32[3,64,270]{2,0,1:T(4,128)S(1)} async-done(((f32[3,64,270]{2,0,1:T(4,128)}), f32[3,64,270]{2,0,1:T(4,128)S(1)}, u32[]{:S(2)}, u32[]{:S(2)}) %all-to-all-start) | async-done | bytes 207392 | tf_op jit(solution)/shard_map/all_to_all | solution.py:102
  46.4 3.9 %all-to-all-start.2 = ((s32[32,12,2]{1,2,0:T(2,128)}), s32[32,12,2]{1,2,0:T(2,128)S(1)}, u32[]{:S(2)}, u32[]{:S(2)}) async-start(s32[32,12,2]{1,2,0:T(2,128)} %copy.136), calls=%async_computation.2 | async-start | bytes 65536 | tf_op jit(solution)/shard_map/all_to_all | solution.py:162
  56.5 0.7 constant_dynamic-update-slice_fusion.30
  57.8 0.7 constant_dynamic-update-slice_fusion.28
  58.5 0.7 constant_dynamic-update-slice_fusion.27
  60.5 0.7 constant_dynamic-update-slice_fusion.24
  62.5 0.7 constant_dynamic-update-slice_fusion.21
  64.6 0.7 constant_dynamic-update-slice_fusion.18
  65.9 0.7 constant_dynamic-update-slice_fusion.16
  67.2 0.7 constant_dynamic-update-slice_fusion.14
  67.9 0.7 constant_dynamic-update-slice_fusion.13
  71.3 0.7 constant_dynamic-update-slice_fusion.8
  72.7 0.7 constant_dynamic-update-slice_fusion.6
  74.0 0.7 constant_dynamic-update-slice_fusion.4
  74.7 0.7 constant_dynamic-update-slice_fusion.3
  77.4 12.2 %all-to-all-start.1 = ((f32[32,3,2,270]{3,2,1,0:T(2,128)}), f32[32,3,2,270]{3,2,1,0:T(2,128)S(1)}, u32[]{:S(2)}, u32[]{:S(2)}) async-start(f32[32,3,2,270]{3,2,1,0:T(2,128)} %constant_dynamic-update-slice_fusion), calls=%async_computation.1 | async-start | bytes 589824 | tf_op jit(solution)/shard_map/all_to_all | solution.py:17
  89.6 1.5 scatter_custom_fusion.1
  91.1 0.8 reshape.148
  91.9 21.8 %all-to-all-done.1 = f32[32,3,2,270]{3,2,1,0:T(2,128)S(1)} async-done(((f32[32,3,2,270]{3,2,1,0:T(2,128)}), f32[32,3,2,270]{3,2,1,0:T(2,128)S(1)}, u32[]{:S(2)}, u32[]{:S(2)}) %all-to-all-start.1) | async-done | bytes 207392 | tf_op jit(solution)/shard_map/all_to_all | solution.py:17
  113.7 3.9 %all-to-all-start.3 = ((f32[32,12,256]{2,1,0:T(8,128)}), f32[32,12,256]{2,1,0:T(8,128)S(1)}, u32[]{:S(2)}, u32[]{:S(2)}) async-start(f32[32,12,256]{2,1,0:T(8,128)} %reshape.148), calls=%async_computation.3 | async-start | bytes 1048576 | tf_op jit(solution)/shard_map/all_to_all | solution.py:155
  118.9 2.8 collective-permute-start
  121.9 21.9 %collective-permute-done.1 = f32[2,64,1]{2,1,0:T(8,128)S(1)} collective-permute-done((f32[2,64,1]{2,1,0:T(8,128)S(1)}, f32[2,64,1]{2,1,0:T(8,128)S(1)}, u32[]{:S(2)}, u32[]{:S(2)}) %collective-permute-start.1) | collective-permute-done | bytes 544 | tf_op jit(solution)/shard_map/ppermute | solution.py:36
  143.9 3.5 %collective-permute-start.3 = (f32[2,1,272]{2,1,0:T(1,128)S(1)}, f32[2,1,272]{2,1,0:T(1,128)S(1)}, u32[]{:S(2)}, u32[]{:S(2)}) collective-permute-start(f32[2,1,272]{2,1,0:T(1,128)S(1)} %get-tuple-element.22), channel_id=1, source_target_pairs={{0,32},{32,64},{64,96},{96,128},{128,160},{160,192},{192,224},{224... | collective-permute-start | bytes 6536 | tf_op jit(solution)/shard_map/ppermute | solution.py:36
  147.4 4.6 %collective-permute-start.2 = (f32[2,1,272]{2,1,0:T(1,128)S(1)}, f32[2,1,272]{2,1,0:T(1,128)S(1)}, u32[]{:S(2)}, u32[]{:S(2)}) collective-permute-start(f32[2,1,272]{2,1,0:T(1,128)S(1)} %get-tuple-element.21), channel_id=1, source_target_pairs={{32,0},{64,32},{96,64},{128,96},{160,128},{192,160},{224,192},{256... | collective-permute-start | bytes 6536 | tf_op jit(solution)/shard_map/ppermute | solution.py:38
  152.1 2.9 %scatter_custom_fusion.2 = f32[64,256]{1,0:T(8,128)S(1)} fusion(s32[384]{0:T(512)S(1)} %get-tuple-element.8, f32[384,256]{1,0:T(8,128)S(1)} %reshape.149, f32[]{:T(128)} %constant.76.clone.1, s32[384]{0:T(512)S(1)} %get-tuple-element.7), kind=kCustom, calls=%fused_computation.33 | custom fusion | flops 294912 | bytes 461824 | tf_op jit(solution)/shard_map/scatter-add | solution.py:169
  155.9 1.1 collective-permute-done.5
  157.0 3.0 %collective-permute-done.4 = f32[1,64,1]{2,1,0:T(8,128)S(1)} collective-permute-done((f32[1,64,1]{2,1,0:T(8,128)S(1)}, f32[1,64,1]{2,1,0:T(8,128)S(1)}, u32[]{:S(2)}, u32[]{:S(2)}) %collective-permute-start.4) | collective-permute-done | bytes 288 | tf_op jit(solution)/shard_map/ppermute | solution.py:36
  160.0 4.5 %collective-permute-start.7 = (f32[1,1,272]{2,1,0:T(1,128)S(1)}, f32[1,1,272]{2,1,0:T(1,128)S(1)}, u32[]{:S(2)}, u32[]{:S(2)}) collective-permute-start(f32[1,1,272]{2,1,0:T(1,128)S(1)} %get-tuple-element.31), channel_id=1, source_target_pairs={{32,0},{64,32},{96,64},{128,96},{160,128},{192,160},{224,192},{256... | collective-permute-start | bytes 3272 | tf_op jit(solution)/shard_map/ppermute | solution.py:38
  164.5 1.9 collective-permute-start.6
  166.5 5.6 %collective-permute-done.6 = f32[1,1,272]{2,1,0:T(1,128)S(1)} collective-permute-done((f32[1,1,272]{2,1,0:T(1,128)S(1)}, f32[1,1,272]{2,1,0:T(1,128)S(1)}, u32[]{:S(2)}, u32[]{:S(2)}) %collective-permute-start.6) | collective-permute-done | bytes 1120 | tf_op jit(solution)/shard_map/ppermute | solution.py:36
  172.6 39.5 %all_to_all.50 = f32[3,64,270]{2,0,1:T(4,128)S(1)} all-to-all(f32[3,64,270]{2,0,1:T(4,128)S(1)} %copy.138), channel_id=1, replica_groups=mesh['band'=16,'lon'=32] {'lon'}, dimensions={1} | all-to-all | bytes 414720 | tf_op jit(solution)/shard_map/all_to_all | solution.py:102
  220.3 27.2 %all_to_all.51 = f32[32,3,2,270]{3,2,1,0:T(2,128)S(1)} all-to-all(f32[32,3,2,270]{3,2,1,0:T(2,128)S(1)} %constant_dynamic-update-slice_fusion.32), channel_id=1, replica_groups=mesh['band'=16,'lon'=32] {'lon'}, dimensions={0} | all-to-all | bytes 414720 | tf_op jit(solution)/shard_map/all_to_all | solution.py:17
  248.0 3.0 %collective-permute-start.8 = (f32[2,64,1]{2,1,0:T(8,128)S(1)}, f32[2,64,1]{2,1,0:T(8,128)S(1)}, u32[]{:S(2)}, u32[]{:S(2)}) collective-permute-start(f32[2,64,1]{2,1,0:T(8,128)S(1)} %get-tuple-element.24), channel_id=1, source_target_pairs={{1,0},{2,1},{3,2},{4,3},{5,4},{6,5},{7,6},{8,7},{9,8},{10,9},{11,1... | collective-permute-start | bytes 1544 | tf_op jit(solution)/shard_map/ppermute | solution.py:38
  251.0 1.9 collective-permute-done.9
  253.0 1.9 collective-permute-start.11
  254.9 6.0 %collective-permute-start.10 = (f32[2,1,272]{2,1,0:T(1,128)S(1)}, f32[2,1,272]{2,1,0:T(1,128)S(1)}, u32[]{:S(2)}, u32[]{:S(2)}) collective-permute-start(f32[2,1,272]{2,1,0:T(1,128)S(1)} %get-tuple-element.19), channel_id=1, source_target_pairs={{32,0},{64,32},{96,64},{128,96},{160,128},{192,160},{224,192},{256... | collective-permute-start | bytes 6536 | tf_op jit(solution)/shard_map/ppermute | solution.py:38
  261.0 1.3 collective-permute-done.10
  262.5 1.8 collective-permute-start.13
  264.3 1.6 collective-permute-done.13
  265.9 3.0 %collective-permute-done.12 = f32[1,64,1]{2,1,0:T(8,128)S(1)} collective-permute-done((f32[1,64,1]{2,1,0:T(8,128)S(1)}, f32[1,64,1]{2,1,0:T(8,128)S(1)}, u32[]{:S(2)}, u32[]{:S(2)}) %collective-permute-start.12) | collective-permute-done | bytes 288 | tf_op jit(solution)/shard_map/ppermute | solution.py:36
  269.0 6.0 %collective-permute-start.15 = (f32[1,1,272]{2,1,0:T(1,128)S(1)}, f32[1,1,272]{2,1,0:T(1,128)S(1)}, u32[]{:S(2)}, u32[]{:S(2)}) collective-permute-start(f32[1,1,272]{2,1,0:T(1,128)S(1)} %get-tuple-element.29), channel_id=1, source_target_pairs={{32,0},{64,32},{96,64},{128,96},{160,128},{192,160},{224,192},{256... | collective-permute-start | bytes 3272 | tf_op jit(solution)/shard_map/ppermute | solution.py:38
  275.0 1.9 collective-permute-start.14
  276.9 5.6 %collective-permute-done.14 = f32[1,1,272]{2,1,0:T(1,128)S(1)} collective-permute-done((f32[1,1,272]{2,1,0:T(1,128)S(1)}, f32[1,1,272]{2,1,0:T(1,128)S(1)}, u32[]{:S(2)}, u32[]{:S(2)}) %collective-permute-start.14) | collective-permute-done | bytes 1120 | tf_op jit(solution)/shard_map/ppermute | solution.py:36
  282.7 0.9 fusion.40
  (147 shorter events, 33.6 us)
Async XLA Ops:
  0.6 1.1 copy-start.1
  2.7 43.7 %all-to-all-start = ((f32[3,64,270]{2,0,1:T(4,128)}), f32[3,64,270]{2,0,1:T(4,128)S(1)}, u32[]{:S(2)}, u32[]{:S(2)}) async-start(f32[3,64,270]{2,0,1:T(4,128)} %copy.129), calls=%async_computation | async-start | bytes 786432 | tf_op jit(solution)/shard_map/all_to_all | solution.py:102
  18.2 0.7 copy-start.3
  18.2 0.7 copy-start.4
  19.0 0.7 copy-start.2
  46.4 31.0 %all-to-all-start.2 = ((s32[32,12,2]{1,2,0:T(2,128)}), s32[32,12,2]{1,2,0:T(2,128)S(1)}, u32[]{:S(2)}, u32[]{:S(2)}) async-start(s32[32,12,2]{1,2,0:T(2,128)} %copy.136), calls=%async_computation.2 | async-start | bytes 65536 | tf_op jit(solution)/shard_map/all_to_all | solution.py:162
  77.4 36.3 %all-to-all-start.1 = ((f32[32,3,2,270]{3,2,1,0:T(2,128)}), f32[32,3,2,270]{3,2,1,0:T(2,128)S(1)}, u32[]{:S(2)}, u32[]{:S(2)}) async-start(f32[32,3,2,270]{3,2,1,0:T(2,128)} %constant_dynamic-update-slice_fusion), calls=%async_computation.1 | async-start | bytes 589824 | tf_op jit(solution)/shard_map/all_to_all | solution.py:17
  113.7 38.3 %all-to-all-start.3 = ((f32[32,12,256]{2,1,0:T(8,128)}), f32[32,12,256]{2,1,0:T(8,128)S(1)}, u32[]{:S(2)}, u32[]{:S(2)}) async-start(f32[32,12,256]{2,1,0:T(8,128)} %reshape.148), calls=%async_computation.3 | async-start | bytes 1048576 | tf_op jit(solution)/shard_map/all_to_all | solution.py:155
  117.6 0.7 copy-start.5
  117.6 0.7 copy-start.6
  118.8 25.0 %collective-permute-start.1 = (f32[2,64,1]{2,1,0:T(8,128)S(1)}, f32[2,64,1]{2,1,0:T(8,128)S(1)}, u32[]{:S(2)}, u32[]{:S(2)}) collective-permute-start(f32[2,64,1]{2,1,0:T(8,128)S(1)} %get-tuple-element.27), channel_id=1, source_target_pairs={{0,1},{1,2},{2,3},{3,4},{4,5},{5,6},{6,7},{7,8},{8,9},{9,10},{10,1... | collective-permute-start | bytes 1544 | tf_op jit(solution)/shard_map/ppermute | solution.py:36
  118.9 24.8 %collective-permute-start = (f32[2,64,1]{2,1,0:T(8,128)S(1)}, f32[2,64,1]{2,1,0:T(8,128)S(1)}, u32[]{:S(2)}, u32[]{:S(2)}) collective-permute-start(f32[2,64,1]{2,1,0:T(8,128)S(1)} %get-tuple-element.26), channel_id=1, source_target_pairs={{1,0},{2,1},{3,2},{4,3},{5,4},{6,5},{7,6},{8,7},{9,8},{10,9},{11,1... | collective-permute-start | bytes 1544 | tf_op jit(solution)/shard_map/ppermute | solution.py:38
  143.9 11.1 %collective-permute-start.3 = (f32[2,1,272]{2,1,0:T(1,128)S(1)}, f32[2,1,272]{2,1,0:T(1,128)S(1)}, u32[]{:S(2)}, u32[]{:S(2)}) collective-permute-start(f32[2,1,272]{2,1,0:T(1,128)S(1)} %get-tuple-element.22), channel_id=1, source_target_pairs={{0,32},{32,64},{64,96},{96,128},{128,160},{160,192},{192,224},{224... | collective-permute-start | bytes 6536 | tf_op jit(solution)/shard_map/ppermute | solution.py:36
  147.4 7.6 %collective-permute-start.2 = (f32[2,1,272]{2,1,0:T(1,128)S(1)}, f32[2,1,272]{2,1,0:T(1,128)S(1)}, u32[]{:S(2)}, u32[]{:S(2)}) collective-permute-start(f32[2,1,272]{2,1,0:T(1,128)S(1)} %get-tuple-element.21), channel_id=1, source_target_pairs={{32,0},{64,32},{96,64},{128,96},{160,128},{192,160},{224,192},{256... | collective-permute-start | bytes 6536 | tf_op jit(solution)/shard_map/ppermute | solution.py:38
  155.4 1.6 collective-permute-start.5
  155.4 4.6 %collective-permute-start.4 = (f32[1,64,1]{2,1,0:T(8,128)S(1)}, f32[1,64,1]{2,1,0:T(8,128)S(1)}, u32[]{:S(2)}, u32[]{:S(2)}) collective-permute-start(f32[1,64,1]{2,1,0:T(8,128)S(1)} %get-tuple-element.34), channel_id=1, source_target_pairs={{0,1},{1,2},{2,3},{3,4},{4,5},{5,6},{6,7},{7,8},{8,9},{9,10},{10,1... | collective-permute-start | bytes 776 | tf_op jit(solution)/shard_map/ppermute | solution.py:36
  160.0 6.5 %collective-permute-start.7 = (f32[1,1,272]{2,1,0:T(1,128)S(1)}, f32[1,1,272]{2,1,0:T(1,128)S(1)}, u32[]{:S(2)}, u32[]{:S(2)}) collective-permute-start(f32[1,1,272]{2,1,0:T(1,128)S(1)} %get-tuple-element.31), channel_id=1, source_target_pairs={{32,0},{64,32},{96,64},{128,96},{160,128},{192,160},{224,192},{256... | collective-permute-start | bytes 3272 | tf_op jit(solution)/shard_map/ppermute | solution.py:38
  164.5 7.6 %collective-permute-start.6 = (f32[1,1,272]{2,1,0:T(1,128)S(1)}, f32[1,1,272]{2,1,0:T(1,128)S(1)}, u32[]{:S(2)}, u32[]{:S(2)}) collective-permute-start(f32[1,1,272]{2,1,0:T(1,128)S(1)} %get-tuple-element.30), channel_id=1, source_target_pairs={{0,32},{32,64},{64,96},{96,128},{128,160},{160,192},{192,224},{224... | collective-permute-start | bytes 3272 | tf_op jit(solution)/shard_map/ppermute | solution.py:36
  166.5 5.7 %copy-start = (s32[64,270]{1,0:T(8,128)S(1)}, s32[64,270]{1,0:T(8,128)}, u32[]{:S(2)}) copy-start(s32[64,270]{1,0:T(8,128)} %param.19) | copy-start | bytes 207364
  248.0 4.9 %collective-permute-start.9 = (f32[2,64,1]{2,1,0:T(8,128)S(1)}, f32[2,64,1]{2,1,0:T(8,128)S(1)}, u32[]{:S(2)}, u32[]{:S(2)}) collective-permute-start(f32[2,64,1]{2,1,0:T(8,128)S(1)} %get-tuple-element.25), channel_id=1, source_target_pairs={{0,1},{1,2},{2,3},{3,4},{4,5},{5,6},{6,7},{7,8},{8,9},{9,10},{10,1... | collective-permute-start | bytes 1544 | tf_op jit(solution)/shard_map/ppermute | solution.py:36
  248.0 4.9 %collective-permute-start.8 = (f32[2,64,1]{2,1,0:T(8,128)S(1)}, f32[2,64,1]{2,1,0:T(8,128)S(1)}, u32[]{:S(2)}, u32[]{:S(2)}) collective-permute-start(f32[2,64,1]{2,1,0:T(8,128)S(1)} %get-tuple-element.24), channel_id=1, source_target_pairs={{1,0},{2,1},{3,2},{4,3},{5,4},{6,5},{7,6},{8,7},{9,8},{10,9},{11,1... | collective-permute-start | bytes 1544 | tf_op jit(solution)/shard_map/ppermute | solution.py:38
  253.0 8.0 %collective-permute-start.11 = (f32[2,1,272]{2,1,0:T(1,128)S(1)}, f32[2,1,272]{2,1,0:T(1,128)S(1)}, u32[]{:S(2)}, u32[]{:S(2)}) collective-permute-start(f32[2,1,272]{2,1,0:T(1,128)S(1)} %get-tuple-element.20), channel_id=1, source_target_pairs={{0,32},{32,64},{64,96},{96,128},{128,160},{160,192},{192,224},{224... | collective-permute-start | bytes 6536 | tf_op jit(solution)/shard_map/ppermute | solution.py:36
  254.9 7.3 %collective-permute-start.10 = (f32[2,1,272]{2,1,0:T(1,128)S(1)}, f32[2,1,272]{2,1,0:T(1,128)S(1)}, u32[]{:S(2)}, u32[]{:S(2)}) collective-permute-start(f32[2,1,272]{2,1,0:T(1,128)S(1)} %get-tuple-element.19), channel_id=1, source_target_pairs={{32,0},{64,32},{96,64},{128,96},{160,128},{192,160},{224,192},{256... | collective-permute-start | bytes 6536 | tf_op jit(solution)/shard_map/ppermute | solution.py:38
  262.5 3.4 %collective-permute-start.13 = (f32[1,64,1]{2,1,0:T(8,128)S(1)}, f32[1,64,1]{2,1,0:T(8,128)S(1)}, u32[]{:S(2)}, u32[]{:S(2)}) collective-permute-start(f32[1,64,1]{2,1,0:T(8,128)S(1)} %get-tuple-element.33), channel_id=1, source_target_pairs={{1,0},{2,1},{3,2},{4,3},{5,4},{6,5},{7,6},{8,7},{9,8},{10,9},{11,1... | collective-permute-start | bytes 776 | tf_op jit(solution)/shard_map/ppermute | solution.py:38
  264.3 4.6 %collective-permute-start.12 = (f32[1,64,1]{2,1,0:T(8,128)S(1)}, f32[1,64,1]{2,1,0:T(8,128)S(1)}, u32[]{:S(2)}, u32[]{:S(2)}) collective-permute-start(f32[1,64,1]{2,1,0:T(8,128)S(1)} %get-tuple-element.32), channel_id=1, source_target_pairs={{0,1},{1,2},{2,3},{3,4},{4,5},{5,6},{6,7},{7,8},{8,9},{9,10},{10,1... | collective-permute-start | bytes 776 | tf_op jit(solution)/shard_map/ppermute | solution.py:36
  269.0 7.9 %collective-permute-start.15 = (f32[1,1,272]{2,1,0:T(1,128)S(1)}, f32[1,1,272]{2,1,0:T(1,128)S(1)}, u32[]{:S(2)}, u32[]{:S(2)}) collective-permute-start(f32[1,1,272]{2,1,0:T(1,128)S(1)} %get-tuple-element.29), channel_id=1, source_target_pairs={{32,0},{64,32},{96,64},{128,96},{160,128},{192,160},{224,192},{256... | collective-permute-start | bytes 3272 | tf_op jit(solution)/shard_map/ppermute | solution.py:38
  275.0 7.6 %collective-permute-start.14 = (f32[1,1,272]{2,1,0:T(1,128)S(1)}, f32[1,1,272]{2,1,0:T(1,128)S(1)}, u32[]{:S(2)}, u32[]{:S(2)}) collective-permute-start(f32[1,1,272]{2,1,0:T(1,128)S(1)} %get-tuple-element.28), channel_id=1, source_target_pairs={{0,32},{32,64},{64,96},{96,128},{128,160},{160,192},{192,224},{224... | collective-permute-start | bytes 3272 | tf_op jit(solution)/shard_map/ppermute | solution.py:36
